TPU v7x, 32 devices: a whole 2x2x4 slice. The times are simulated.
32 devices in a mesh: ctx: 8 (over z, y), grp: 4 (over x, core).
Axes of the slice: x: 2, y: 2, z: 4, core: 2. Of those that a mesh axis runs over, the one named last changes fastest.
Arguments:
- tokens: bfloat16 [4, 512, 8192], P('grp', 'ctx'), may hold values from -6 to 6
- queries: bfloat16 [4, 512, 4096], P('grp', 'ctx'), may hold values from -32 to 32
- key_value_weight: bfloat16 [8192, 1024], P('grp'), may hold values from -0.0625 to 0.0625
- adapter_down_weight: bfloat16 [8192, 128], P('grp'), may hold values from -0.0625 to 0.0625
- adapter_up_weight: bfloat16 [2, 64, 512], replicated, may hold values from -0.75 to 0.75
- tile_request_mask: int32 [4, 4, 4], P('grp'), may hold values 0 or 1
- lengths: int32 [4], P('grp'), may hold values from 128 to 512, as said below
- page_lookup_table: int32 [4, 128], P(None, 'ctx'), may hold values from 0 to 63, as said below
Outputs:
- attended: bfloat16 [4, 512, 4096], P('grp', 'ctx')
- decode_cache: bfloat16 [4, 128, 4, 1024], P('grp', 'ctx')
Inputs may be any that keep to these rules, and one draw needn't show every extreme that they name: `page_lookup_table`: pages of positions held by one index of ctx go to decode-cache rows of that same index. Every decode group receives exactly 16 pages into distinct slots from the pages of each index of ctx. From the pages of one rollout on one index of ctx, at most max(2, ceil(4)) go to one group, and exactly that many to some group. `lengths`: some rollout has all 512 positions live.
All inputs are finite; a program needn't handle non-finite values. No bound on the sum of `tile_request_mask` on one device may be relied on, other than what follows from the above.
Results may differ from a plain program's by a relative error of at most 0.028.
Values may be sent and summed in bfloat16 or wider, within the bound.
A program may use at most 64 MiB of HBM per device.

v0:
```python
import jax
import jax.numpy as jnp
from jax import lax
from jax.sharding import PartitionSpec as P

HEAD_SIZE = 128
HQ = 32
KEY_VALUE_HEADS = 4
PAGE = 4
TILE = 128
THETA = 500000.0
ADAPTER_SCALE = 0.5


def rotate(key_rows, token_positions):
    half_split = HEAD_SIZE // 2
    freq = THETA ** (-(2.0 * jnp.arange(half_split, dtype=jnp.float32)) / HEAD_SIZE)
    angle = token_positions.astype(jnp.float32)[:, None] * freq[None, :]
    cosine = jnp.cos(angle)[:, None, :]
    sine = jnp.sin(angle)[:, None, :]
    first = key_rows[..., :half_split]
    second = key_rows[..., half_split:]
    return jnp.concatenate([first * cosine - second * sine, second * cosine + first * sine], -1)


def send_pages(own, page_lookup_table, groups):
    column_width = own.shape[1]
    ppd = own.shape[0] // PAGE
    most = max(2, -(-ppd // groups))
    me = lax.axis_index("grp")
    dest = page_lookup_table // ppd
    slot = page_lookup_table % ppd
    earlier = jnp.arange(ppd)[:, None] > jnp.arange(ppd)[None, :]
    same = dest[:, :, None] == dest[:, None, :]
    order = jnp.sum(same & earlier[None], axis=2)
    my_dest = lax.dynamic_index_in_dim(dest, me, 0, keepdims=False)
    my_order = lax.dynamic_index_in_dim(order, me, 0, keepdims=False)
    pick = (my_dest[None, None, :] == jnp.arange(groups)[:, None, None]) & (
        my_order[None, None, :] == jnp.arange(most)[None, :, None]
    )
    pages = own.reshape(ppd, PAGE * column_width)
    outgoing = jnp.einsum(
        "gck,kf->gcf", pick.astype(jnp.bfloat16), pages, preferred_element_type=jnp.float32
    ).astype(jnp.bfloat16)
    incoming = lax.all_to_all(outgoing, "grp", split_axis=0, concat_axis=0, tiled=True)
    place = (
        (dest[None, :, None, :] == me)
        & (order[None, :, None, :] == jnp.arange(most)[None, None, :, None])
        & (slot[None, :, None, :] == jnp.arange(ppd)[:, None, None, None])
    )
    place = jnp.any(place, axis=3).reshape(ppd, groups * most)
    cache = jnp.dot(
        place.astype(jnp.bfloat16),
        incoming.reshape(groups * most, PAGE * column_width),
        preferred_element_type=jnp.float32,
    )
    return cache.astype(jnp.bfloat16).reshape(1, ppd, PAGE, column_width)


def local(
    tokens,
    queries,
    key_value_weight,
    adapter_down_weight,
    adapter_up_weight,
    tile_request_mask,
    lengths,
    page_lookup_table,
):
    groups = lax.axis_size("grp")
    tok = tokens.shape[1]
    column_width = key_value_weight.shape[1]
    half_split = column_width // 2
    rank_count = adapter_up_weight.shape[1]
    group = HQ // KEY_VALUE_HEADS
    ctx_pos = lax.axis_index("ctx")
    token_positions = ctx_pos * tok + jnp.arange(tok, dtype=jnp.int32)
    mixed_output = lax.all_to_all(tokens[0], "grp", split_axis=1, concat_axis=0, tiled=True)
    summed_output = lax.psum_scatter(
        jnp.concatenate(
            [
                jnp.dot(mixed_output, key_value_weight, preferred_element_type=jnp.float32),
                jnp.dot(mixed_output, adapter_down_weight, preferred_element_type=jnp.float32),
            ],
            1,
        ).astype(jnp.bfloat16),
        "grp",
        scatter_dimension=0,
        tiled=True,
    ).astype(jnp.float32)
    low_rank_state = summed_output[:, column_width:].astype(jnp.bfloat16)
    key_rows = summed_output[:, :half_split] + ADAPTER_SCALE * jnp.dot(
        low_rank_state[:, :rank_count], adapter_up_weight[0], preferred_element_type=jnp.float32
    )
    value_rows = summed_output[:, half_split:column_width] + ADAPTER_SCALE * jnp.dot(
        low_rank_state[:, rank_count:], adapter_up_weight[1], preferred_element_type=jnp.float32
    )
    key_rows = rotate(key_rows.reshape(tok, KEY_VALUE_HEADS, HEAD_SIZE), token_positions).reshape(
        tok, half_split
    )
    own = jnp.concatenate([key_rows, value_rows], 1).astype(jnp.bfloat16)
    decode_cache = send_pages(own, page_lookup_table, groups)
    query_heads = queries[0].reshape(tok, KEY_VALUE_HEADS, group, HEAD_SIZE)
    scale = 1.0 / HEAD_SIZE**0.5
    tiles = tile_request_mask.shape[1]
    tile_ids = jnp.arange(tiles, dtype=jnp.int32)
    query_tile = token_positions // TILE
    query_onehot = (query_tile[:, None] == tile_ids[None, :]).astype(jnp.float32)
    live_rows = jnp.dot(query_onehot, tile_request_mask[0].astype(jnp.float32))
    length = lengths[0]
    initial = (
        jnp.full((KEY_VALUE_HEADS, group, tok, 1), -1e30, jnp.float32),
        jnp.zeros((KEY_VALUE_HEADS, group, tok, 1), jnp.float32),
        jnp.zeros((KEY_VALUE_HEADS, group, tok, HEAD_SIZE), jnp.float32),
    )
    state = initial
    piece = lax.all_gather(own, "ctx", axis=0, tiled=True)
    count = piece.shape[0]
    blk = 512
    blocks = piece.reshape(count // blk, blk, column_width)

    def inner(carry, item):
        offset, block = item
        peak, total, acc = carry
        kpos = offset * blk + jnp.arange(blk, dtype=jnp.int32)
        key_block = block[:, :half_split].reshape(blk, KEY_VALUE_HEADS, HEAD_SIZE)
        value_block = (
            block[:, half_split:].reshape(blk, KEY_VALUE_HEADS, HEAD_SIZE).astype(jnp.float32)
        )
        score = (
            jnp.einsum("qhgd,khd->hgqk", query_heads, key_block, preferred_element_type=jnp.float32)
            * scale
        )
        key_tile = kpos // TILE
        key_onehot = (key_tile[:, None] == tile_ids[None, :]).astype(jnp.float32)
        live = jnp.dot(live_rows, key_onehot.T) > 0.5
        live = live | (query_tile[:, None] == key_tile[None, :])
        allowed = (kpos[None, :] <= token_positions[:, None]) & (kpos[None, :] >= 0) & live & (
            kpos[None, :] < length
        ) | (kpos[None, :] == token_positions[:, None])
        masked = jnp.where(allowed, score, -1e30)
        new_peak = jnp.maximum(peak, jnp.max(masked, axis=-1, keepdims=True))
        expo = jnp.where(allowed, jnp.exp(masked - new_peak), 0.0)
        factor = jnp.exp(peak - new_peak)
        total = total * factor + jnp.sum(expo, axis=-1, keepdims=True)
        acc = acc * factor + jnp.einsum(
            "hgqk,khd->hgqd", expo, value_block, preferred_element_type=jnp.float32
        )
        return ((new_peak, total, acc), None)

    offsets = jnp.arange(count // blk, dtype=jnp.int32)
    state, _ = lax.scan(inner, state, (offsets, blocks))
    peak, total, acc = state
    out = acc / total
    out = jnp.transpose(out, (2, 0, 1, 3)).reshape(tok, HQ * HEAD_SIZE)
    out = jnp.where((token_positions < length)[:, None], out, 0.0)
    attended = out.astype(jnp.bfloat16)[None]
    return (attended, decode_cache)


def solution(mesh):
    in_specs = (
        P("grp", "ctx", None),
        P("grp", "ctx", None),
        P("grp", None),
        P("grp", None),
        P(),
        P("grp", None, None),
        P("grp"),
        P(None, "ctx"),
    )
    out_specs = (P("grp", "ctx", None), P("grp", "ctx", None, None))
    return jax.shard_map(local, mesh=mesh, in_specs=in_specs, out_specs=out_specs, check_vma=False)
```

profile of v0, /device:TPU:0, one launch (start us, length us, event | category | flops | bytes accessed | tf_op | source)
XLA Modules:
  0.0 115.5 jit_solution(12051520847819461086)
XLA Ops:
  7.2 0.0 copy-start
  7.2 1.9 %all_to_all.17 = bf16[64,4,2048]{2,1,0:T(4,128)(2,1)S(1)} reshape(bf16[1,64,8192]{2,1,0:T(8,128)(2,1)} %param.8) | data formatting | bytes 2097152 | tf_op jit(solution)/shard_map/all_to_all | solution.py:78
  9.1 1.5 %copy.31 = bf16[64,4,2048]{2,0,1:T(8,128)(2,1)} copy(bf16[64,4,2048]{2,1,0:T(4,128)(2,1)S(1)} %all_to_all.17) | data formatting | bytes 2097152 | tf_op jit(solution)/shard_map/all_to_all | solution.py:78
  10.6 4.2 %all-to-all-start = ((bf16[64,4,2048]{2,0,1:T(8,128)(2,1)}), bf16[64,4,2048]{2,0,1:T(8,128)(2,1)S(1)}, u32[]{:S(2)}, u32[]{:S(2)}) async-start(bf16[64,4,2048]{2,0,1:T(8,128)(2,1)} %copy.31), calls=%async_computation | async-start | bytes 2097152 | tf_op jit(solution)/shard_map/all_to_all | solution.py:78
  14.8 0.0 reduce-scatter.2.cloned.1.call-start
  14.9 14.4 %all-to-all-done = bf16[64,4,2048]{2,0,1:T(8,128)(2,1)S(1)} async-done(((bf16[64,4,2048]{2,0,1:T(8,128)(2,1)}), bf16[64,4,2048]{2,0,1:T(8,128)(2,1)S(1)}, u32[]{:S(2)}, u32[]{:S(2)}) %all-to-all-start) | async-done | bytes 1048608 | tf_op jit(solution)/shard_map/all_to_all | solution.py:78
  29.3 0.0 copy-done
  29.3 0.4 convolution_convert_fusion.2
  29.7 0.0 copy-start.3
  29.8 0.0 copy-start.2
  29.8 0.0 copy-start.1
  29.8 3.5 %convolution_convert_fusion.1 = bf16[256,1024]{1,0:T(8,128)(2,1)S(1)} fusion(bf16[256,2048]{1,0:T(8,128)(2,1)S(1)} %bitcast.71, bf16[2048,1024]{1,0:T(8,128)(2,1)} %param.10), kind=kOutput, calls=%fused_computation.15 | convolution fusion | flops 1074003968 | bytes 5767168 | tf_op jit(solution)/shard_map/dot_general | solution.py:82
  33.3 0.0 copy-start.4
  33.3 0.9 pad_maximum_fusion
  34.2 0.0 reduce-scatter.2.cloned.1.call-update
  34.2 0.0 all-gather.2.cloned.1.call-start
  34.9 0.0 copy-done.3
  35.0 0.2 convert_reduce_fusion
  35.2 0.2 multiply_cosine_fusion
  35.4 22.0 %reduce-scatter.2.cloned.1.call-done = bf16[64,1152]{1,0:T(8,128)(2,1)} async-done(((bf16[256,1152]{1,0:T(8,128)(2,1)}), bf16[64,1152]{1,0:T(8,128)(2,1)}) %reduce-scatter.2.cloned.1.call-update) | async-done | bytes 147472 | tf_op jit(solution)/shard_map/reduce_scatter | solution.py:79
  57.4 0.9 convert_element_type.53
  58.4 0.0 copy-done.2
  58.4 0.9 fusion.12
  59.3 0.2 multiply_subtract_fusion
  59.5 0.1 pad_maximum_fusion.1
  59.6 0.9 fusion.11
  60.5 0.7 maximum_convert_fusion
  61.2 0.0 all-gather.2.cloned.1.call-update
  61.2 0.0 copy-done.1
  61.2 0.1 copy.45
  61.4 0.4 and_reduce_fusion
  61.8 0.0 copy-done.4
  61.8 0.4 fusion.16
  62.2 1.0 reshape.298
  63.2 0.8 convolution_convert_fusion
  64.1 3.3 %all-to-all-start.1 = ((bf16[4,4,4096]{2,1,0:T(4,128)(2,1)}), bf16[4,4,4096]{2,1,0:T(4,128)(2,1)S(1)}, u32[]{:S(2)}, u32[]{:S(2)}) async-start(bf16[4,4,4096]{2,1,0:T(4,128)(2,1)} %convolution_convert_fusion), calls=%async_computation.2 | async-start | bytes 262144 | tf_op jit(solution)/shard_map/all_to_all | solution.py:45
  67.4 4.6 %all-to-all-done.1 = bf16[4,4,4096]{2,1,0:T(4,128)(2,1)S(1)} async-done(((bf16[4,4,4096]{2,1,0:T(4,128)(2,1)}), bf16[4,4,4096]{2,1,0:T(4,128)(2,1)S(1)}, u32[]{:S(2)}, u32[]{:S(2)}) %all-to-all-start.1) | async-done | bytes 131104 | tf_op jit(solution)/shard_map/all_to_all | solution.py:45
  72.0 0.2 fusion
  72.2 0.7 reshape.295
  73.0 28.6 %all-gather.2.cloned.1.call-done = bf16[512,1024]{1,0:T(8,128)(2,1)} async-done(((bf16[64,1024]{1,0:T(8,128)(2,1)}), bf16[512,1024]{1,0:T(8,128)(2,1)}) %all-gather.2.cloned.1.call-update) | async-done | bytes 1048592 | tf_op jit(solution)/shard_map/all_gather | solution.py:117
  101.6 1.3 %fusion.49 = (bf16[512,512]{1,0:T(8,128)(2,1)S(1)}, bf16[512,512]{1,0:T(8,128)(2,1)S(1)}) fusion(bf16[512,1024]{1,0:T(8,128)(2,1)} %all-gather.2.cloned.1.call-done), kind=kLoop, calls=%fused_computation.99 | loop fusion | bytes 2097152 | tf_op jit(solution)/shard_map/while/body/eval_jaxpr/slice | solution.py:128
  102.9 0.1 reshape.293
  103.0 0.1 reshape.292
  103.1 1.0 fusion.1
  104.2 1.3 %fusion.2 = f32[4,8,64]{2,1,0:T(8,128)S(1)} fusion(f32[4,512,64,8]{1,2,3,0:T(8,128)S(1)} %get-tuple-element.46, f32[4,8,64]{2,1,0:T(8,128)S(1)} %get-tuple-element.31, pred[64,512]{1,0:T(8,128)(4,1)S(1)} %fusion.16), kind=kLoop, calls=%fused_computation.6 | loop fusion | flops 5240832 | bytes 4243456 | tf_op jit(solution)/shard_map/while/body/eval_jaxpr/reduce_sum | solution.py:145
  105.5 1.6 %fusion.19 = bf16[64,4,8,128]{3,0,2,1:T(8,128)(2,1)S(1)} fusion(f32[4,512,64,8]{1,2,3,0:T(8,128)S(1)} %get-tuple-element.46, f32[4,8,64]{2,1,0:T(8,128)S(1)} %get-tuple-element.31, pred[64,512]{1,0:T(8,128)(4,1)S(1)} %fusion.16, bf16[512,4,128,1]{2,1,0,3:T(4,128)(2,1)S(1)} %bitcast.74, f32[64,4,8]{0,2,1:T(8,128)S(1)} %bitcast_add_fusion, ...), kind=kOutput, calls=%fused_computation.28 | convolution fusion | flops 273416192 | bytes 5300224 | tf_op jit(solution)/shard_map/while/body/eval_jaxpr/hgqk,khd->hgqd/dot_general | solution.py:146
  107.1 0.3 copy.36
  107.5 0.2 reshape.294
  107.7 1.0 select_convert_fusion
  (18 shorter events, 0.2 us)
Async XLA Ops:
  7.2 22.1 %copy-start = (bf16[2048,128]{1,0:T(8,128)(2,1)S(1)}, bf16[2048,128]{1,0:T(8,128)(2,1)}, u32[]{:S(2)}) copy-start(bf16[2048,128]{1,0:T(8,128)(2,1)} %param.11) | copy-start | bytes 1572868
  10.6 18.7 %all-to-all-start = ((bf16[64,4,2048]{2,0,1:T(8,128)(2,1)}), bf16[64,4,2048]{2,0,1:T(8,128)(2,1)S(1)}, u32[]{:S(2)}, u32[]{:S(2)}) async-start(bf16[64,4,2048]{2,0,1:T(8,128)(2,1)} %copy.31), calls=%async_computation | async-start | bytes 2097152 | tf_op jit(solution)/shard_map/all_to_all | solution.py:78
  14.8 42.6 %reduce-scatter.2.cloned.1.call-start = ((), (), s32[]{:S(2)}) async-start(), calls=%async_computation.3 | async-start | bytes 737280 | tf_op jit(solution)/shard_map/reduce_scatter | solution.py:79
  29.7 5.2 %copy-start.3 = (s32[4,16]{1,0:T(4,128)S(1)}, s32[4,16]{1,0:T(4,128)}, u32[]{:S(2)}) copy-start(s32[4,16]{1,0:T(4,128)} %param.15) | copy-start | bytes 772
  29.8 28.6 %copy-start.2 = (bf16[2,64,512]{2,1,0:T(8,128)(2,1)S(1)}, bf16[2,64,512]{2,1,0:T(8,128)(2,1)}, u32[]{:S(2)}) copy-start(bf16[2,64,512]{2,1,0:T(8,128)(2,1)} %param.12) | copy-start | bytes 393220
  29.8 31.5 %copy-start.1 = (bf16[1,64,4096]{2,1,0:T(8,128)(2,1)S(1)}, bf16[1,64,4096]{2,1,0:T(8,128)(2,1)}, u32[]{:S(2)}) copy-start(bf16[1,64,4096]{2,1,0:T(8,128)(2,1)} %param.9) | copy-start | bytes 1572868
  33.3 28.5 %copy-start.4 = (s32[1,4,4]{2,1,0:T(4,128)S(1)}, s32[1,4,4]{2,1,0:T(4,128)}, u32[]{:S(2)}) copy-start(s32[1,4,4]{2,1,0:T(4,128)} %param.13) | copy-start | bytes 196
  34.2 67.4 %all-gather.2.cloned.1.call-start = ((), (), s32[]{:S(2)}) async-start(), calls=%async_computation.4 | async-start | bytes 1179648 | tf_op jit(solution)/shard_map/all_gather | solution.py:117
  64.1 7.9 %all-to-all-start.1 = ((bf16[4,4,4096]{2,1,0:T(4,128)(2,1)}), bf16[4,4,4096]{2,1,0:T(4,128)(2,1)S(1)}, u32[]{:S(2)}, u32[]{:S(2)}) async-start(bf16[4,4,4096]{2,1,0:T(4,128)(2,1)} %convolution_convert_fusion), calls=%async_computation.2 | async-start | bytes 262144 | tf_op jit(solution)/shard_map/all_to_all | solution.py:45
Sparse Core Ops, SparseCore 0:
  34.3 23.0 reduce-scatter.1
  61.3 40.2 all-gather.1
where the time goes:
time: 116 us; the launch traced here: 115 us
  waiting for transfers between devices  69.7 us (60%)
  between operations  15 us (13%)
  matrix products  9.79 us (8%)
  starting transfers between devices  7.58 us (7%)
  local copies, waits for them, and re-layouts  7.46 us (6%)
  other arithmetic  5.95 us (5%)
    all_gather x1, waiting for transfers between devices, local(): piece = lax.all_gather(own, 'ctx', axis=0, tiled=True)  28.6 us
    reduce_scatter x1, waiting for transfers between devices, local(): lax.psum_scatter(jnp.concatenate([jnp.dot(mixed_output, key_value_weight,...  22 us
    all_to_all x1, waiting for transfers between devices, local(): lax.all_to_all(tokens[0], 'grp', split_axis=1, concat_axis=0, tiled=True)  14.4 us
    all_to_all x1, waiting for transfers between devices, send_pages(): lax.all_to_all(outgoing, 'grp', split_axis=0, concat_axis=0, tiled=True)  4.58 us
    all_to_all x1, starting transfers between devices, local(): lax.all_to_all(tokens[0], 'grp', split_axis=1, concat_axis=0, tiled=True)  4.21 us
    dot_general x1, matrix products, local(): jnp.dot(mixed_output, key_value_weight, preferred_element_type=jnp.float32)  3.5 us
    all_to_all x2, local copies, waits for them, and re-layouts, local(): lax.all_to_all(tokens[0], 'grp', split_axis=1, concat_axis=0, tiled=True)  3.45 us
    all_to_all x1, starting transfers between devices, send_pages(): lax.all_to_all(outgoing, 'grp', split_axis=0, concat_axis=0, tiled=True)  3.33 us
  transfers between devices with their start and end apart: 4, of which 4 were waited for; matrix products, arithmetic and copies ran while one was open for 4% of the time, Pallas kernels for 0%

commit v1 on v0

--- a/solution.py
+++ b/solution.py
@@ -10,6 +10,28 @@
 TILE = 128
 THETA = 500000.0
 ADAPTER_SCALE = 0.5
+
+
+def joined_along(blocks, dim):
+    shape = list(blocks.shape[1:])
+    shape[dim] *= blocks.shape[0]
+    return jnp.moveaxis(blocks, 0, dim).reshape(shape)
+
+
+def gather_around(x, axis, dim):
+    size = lax.axis_size(axis)
+    pairs = [(i, (i + 1) % size) for i in range(size)]
+    back = [(b, a) for a, b in pairs]
+    lower, upper = ([], [])
+    for lap in range(size - 1):
+        if lap % 2 == 0:
+            lower.append(lax.ppermute(lower[-1] if lower else x, axis, pairs))
+        else:
+            upper.append(lax.ppermute(upper[-1] if upper else x, axis, back))
+    blocks = jnp.stack([*lower[::-1], x, *upper])
+    shift = lax.axis_index(axis) - len(lower)
+    blocks = blocks[(jnp.arange(size) - shift) % size]
+    return joined_along(blocks, dim)
 
 
 def rotate(key_rows, token_positions):
@@ -114,7 +136,7 @@
         jnp.zeros((KEY_VALUE_HEADS, group, tok, HEAD_SIZE), jnp.float32),
     )
     state = initial
-    piece = lax.all_gather(own, "ctx", axis=0, tiled=True)
+    piece = gather_around(own, "ctx", 0)
     count = piece.shape[0]
     blk = 512
     blocks = piece.reshape(count // blk, blk, column_width)

time: 116 us -> 110 us (0.948)
  waiting for transfers between devices: 69.7 us -> 49.7 us
  starting transfers between devices: 7.58 us -> 23.9 us
  local copies, waits for them, and re-layouts: 7.46 us -> 6.27 us
    all_gather x1 -> x0, waiting for transfers between devices: 28.6 us -> none  [local(): piece = lax.all_gather(own, 'ctx', axis=0, tiled=True)]
    ppermute x0 -> x7, starting transfers between devices: none -> 16.4 us  [the longest x3 14.8 us: gather_around(): upper.append(lax.ppermute(upper[-1] if upper else x, axis, back))]
    ppermute x0 -> x7, waiting for transfers between devices: none -> 13.6 us  [the longest x4 8.84 us: gather_around(): lower.append(lax.ppermute(lower[-1] if lower else x, axis, pairs))]
    all_to_all x1, waiting for transfers between devices: 4.58 us -> 0.01 us  [send_pages(): lax.all_to_all(outgoing, 'grp', split_axis=0, concat_axis=0, tiled=True)]
    slice x1, local copies, waits for them, and re-layouts: 1.27 us -> 0.08 us  [inner(): key_block = block[:, :half_split].reshape(blk, KEY_VALUE_HEADS, HEAD_SIZE)]
  transfers between devices with their start and end apart: 4 -> 10, of which waited for: 4 -> 6; matrix products, arithmetic and copies ran while one was open for 4% -> 3% of each run, Pallas kernels for 0% -> 0%
where the time goes in v1:
time: 110 us
  waiting for transfers between devices  49.7 us (45%)
  starting transfers between devices  23.9 us (22%)
  between operations  15.1 us (14%)
  matrix products  9.72 us (9%)
  local copies, waits for them, and re-layouts  6.27 us (6%)
  other arithmetic  5.33 us (5%)
    reduce_scatter x1, waiting for transfers between devices, local(): lax.psum_scatter(jnp.concatenate([jnp.dot(mixed_output, key_value_weight,...  22.5 us
    ppermute x3, starting transfers between devices, gather_around(): upper.append(lax.ppermute(upper[-1] if upper else x, axis, back))  14.8 us
    all_to_all x1, waiting for transfers between devices, local(): lax.all_to_all(tokens[0], 'grp', split_axis=1, concat_axis=0, tiled=True)  13.5 us
    ppermute x4, waiting for transfers between devices, gather_around(): lower.append(lax.ppermute(lower[-1] if lower else x, axis, pairs))  8.84 us
    ppermute x3, waiting for transfers between devices, gather_around(): upper.append(lax.ppermute(upper[-1] if upper else x, axis, back))  4.77 us
    all_to_all x1, starting transfers between devices, local(): lax.all_to_all(tokens[0], 'grp', split_axis=1, concat_axis=0, tiled=True)  4.21 us
    dot_general x1, matrix products, local(): jnp.dot(mixed_output, key_value_weight, preferred_element_type=jnp.float32)  3.47 us
    all_to_all x2, local copies, waits for them, and re-layouts, local(): lax.all_to_all(tokens[0], 'grp', split_axis=1, concat_axis=0, tiled=True)  3.46 us
  transfers between devices with their start and end apart: 10, of which 6 were waited for; matrix products, arithmetic and copies ran while one was open for 3% of the time, Pallas kernels for 0%

profile of v1, /device:TPU:0, one launch (start us, length us, event | category | flops | bytes accessed | tf_op | source)
XLA Modules:
  0.0 109.9 jit_solution(952594658373295689)
XLA Ops:
  7.2 0.0 copy-start
  7.2 0.0 copy-start.3
  7.2 1.9 %all_to_all.17 = bf16[64,4,2048]{2,1,0:T(4,128)(2,1)S(1)} reshape(bf16[1,64,8192]{2,1,0:T(8,128)(2,1)} %param.8) | data formatting | bytes 2097152 | tf_op jit(solution)/shard_map/all_to_all | solution.py:100
  9.1 1.6 %copy.35 = bf16[64,4,2048]{2,0,1:T(8,128)(2,1)} copy(bf16[64,4,2048]{2,1,0:T(4,128)(2,1)S(1)} %all_to_all.17) | data formatting | bytes 2097152 | tf_op jit(solution)/shard_map/all_to_all | solution.py:100
  10.7 4.2 %all-to-all-start = ((bf16[64,4,2048]{2,0,1:T(8,128)(2,1)}), bf16[64,4,2048]{2,0,1:T(8,128)(2,1)S(1)}, u32[]{:S(2)}, u32[]{:S(2)}) async-start(bf16[64,4,2048]{2,0,1:T(8,128)(2,1)} %copy.35), calls=%async_computation | async-start | bytes 2097152 | tf_op jit(solution)/shard_map/all_to_all | solution.py:100
  14.9 0.0 reduce-scatter.2.cloned.1.call-start
  15.6 0.0 copy-done.3
  15.6 0.2 convert_reduce_fusion
  15.9 13.5 %all-to-all-done = bf16[64,4,2048]{2,0,1:T(8,128)(2,1)S(1)} async-done(((bf16[64,4,2048]{2,0,1:T(8,128)(2,1)}), bf16[64,4,2048]{2,0,1:T(8,128)(2,1)S(1)}, u32[]{:S(2)}, u32[]{:S(2)}) %all-to-all-start) | async-done | bytes 1048608 | tf_op jit(solution)/shard_map/all_to_all | solution.py:100
  29.3 0.0 copy-done
  29.3 0.4 convolution_convert_fusion.2
  29.8 0.0 copy-start.4
  29.8 0.0 copy-start.2
  29.8 3.5 %convolution_convert_fusion.1 = bf16[256,1024]{1,0:T(8,128)(2,1)S(1)} fusion(bf16[256,2048]{1,0:T(8,128)(2,1)S(1)} %bitcast.102, bf16[2048,1024]{1,0:T(8,128)(2,1)} %param.10), kind=kOutput, calls=%fused_computation.16 | convolution fusion | flops 1074003968 | bytes 5767168 | tf_op jit(solution)/shard_map/dot_general | solution.py:104
  33.3 0.0 copy-start.1
  33.3 0.9 pad_maximum_fusion
  34.1 0.0 reduce-scatter.2.cloned.1.call-update
  34.2 0.0 copy-done.4
  34.2 0.4 fusion.16
  34.7 0.2 multiply_cosine_fusion
  34.9 22.5 %reduce-scatter.2.cloned.1.call-done = bf16[64,1152]{1,0:T(8,128)(2,1)} async-done(((bf16[256,1152]{1,0:T(8,128)(2,1)}), bf16[64,1152]{1,0:T(8,128)(2,1)}) %reduce-scatter.2.cloned.1.call-update) | async-done | bytes 147472 | tf_op jit(solution)/shard_map/reduce_scatter | solution.py:101
  57.4 0.9 convert_element_type.60
  58.4 0.0 copy-done.2
  58.4 0.9 fusion.12
  59.3 0.2 multiply_subtract_fusion
  59.5 0.1 pad_maximum_fusion.1
  59.6 0.9 fusion.11
  60.6 1.5 %collective-permute-start = (bf16[64,1024]{1,0:T(8,128)(2,1)S(1)}, bf16[64,1024]{1,0:T(8,128)(2,1)S(1)}, u32[]{:S(2)}, u32[]{:S(2)}) collective-permute-start(bf16[64,1024]{1,0:T(8,128)(2,1)S(1)} %maximum_convert_fusion), channel_id=1, source_target_pairs={{0,4},{4,8},{8,12},{12,16},{16,20},{20,24},{24,28},{28,0},{1,5},{5... | collective-permute-start | bytes 393224 | tf_op jit(solution)/shard_map/ppermute | solution.py:28
  62.1 6.4 %collective-permute-done = bf16[64,1024]{1,0:T(8,128)(2,1)S(1)} collective-permute-done((bf16[64,1024]{1,0:T(8,128)(2,1)S(1)}, bf16[64,1024]{1,0:T(8,128)(2,1)S(1)}, u32[]{:S(2)}, u32[]{:S(2)}) %collective-permute-start) | collective-permute-done | bytes 131104 | tf_op jit(solution)/shard_map/ppermute | solution.py:28
  68.5 0.0 collective-permute-start.1
  68.5 0.0 copy-done.1
  68.6 0.1 copy.53
  68.7 0.4 and_reduce_fusion
  69.0 0.1 reshape.385
  69.1 4.8 %collective-permute-start.4 = (bf16[64,1024]{1,0:T(8,128)(2,1)S(1)}, bf16[64,1024]{1,0:T(8,128)(2,1)S(1)}, u32[]{:S(2)}, u32[]{:S(2)}) collective-permute-start(bf16[64,1024]{1,0:T(8,128)(2,1)S(1)} %maximum_convert_fusion), channel_id=1, source_target_pairs={{4,0},{8,4},{12,8},{16,12},{20,16},{24,20},{28,24},{0,28},{5,1},{9... | collective-permute-start | bytes 393224 | tf_op jit(solution)/shard_map/ppermute | solution.py:30
  73.9 2.4 %collective-permute-done.1 = bf16[64,1024]{1,0:T(8,128)(2,1)S(1)} collective-permute-done((bf16[64,1024]{1,0:T(8,128)(2,1)S(1)}, bf16[64,1024]{1,0:T(8,128)(2,1)S(1)}, u32[]{:S(2)}, u32[]{:S(2)}) %collective-permute-start.1) | collective-permute-done | bytes 131104 | tf_op jit(solution)/shard_map/ppermute | solution.py:28
  76.3 0.0 collective-permute-start.2
  76.3 0.8 convolution_convert_fusion
  77.1 3.3 %all-to-all-start.1 = ((bf16[4,4,4096]{2,1,0:T(4,128)(2,1)}), bf16[4,4,4096]{2,1,0:T(4,128)(2,1)S(1)}, u32[]{:S(2)}, u32[]{:S(2)}) async-start(bf16[4,4,4096]{2,1,0:T(4,128)(2,1)} %convolution_convert_fusion), calls=%async_computation.2 | async-start | bytes 262144 | tf_op jit(solution)/shard_map/all_to_all | solution.py:67
  80.5 0.0 collective-permute-done.4
  80.5 4.8 %collective-permute-start.5 = (bf16[64,1024]{1,0:T(8,128)(2,1)S(1)}, bf16[64,1024]{1,0:T(8,128)(2,1)S(1)}, u32[]{:S(2)}, u32[]{:S(2)}) collective-permute-start(bf16[64,1024]{1,0:T(8,128)(2,1)S(1)} %collective-permute-done.4), channel_id=1, source_target_pairs={{4,0},{8,4},{12,8},{16,12},{20,16},{24,20},{28,24},{0,28},{5,1},{9... | collective-permute-start | bytes 393224 | tf_op jit(solution)/shard_map/ppermute | solution.py:30
  85.3 0.0 collective-permute-done.2
  85.3 0.0 collective-permute-start.3
  85.3 0.0 all-to-all-done.1
  85.3 0.2 fusion
  85.6 0.7 reshape.374
  86.3 2.4 %collective-permute-done.5 = bf16[64,1024]{1,0:T(8,128)(2,1)S(1)} collective-permute-done((bf16[64,1024]{1,0:T(8,128)(2,1)S(1)}, bf16[64,1024]{1,0:T(8,128)(2,1)S(1)}, u32[]{:S(2)}, u32[]{:S(2)}) %collective-permute-start.5) | collective-permute-done | bytes 131104 | tf_op jit(solution)/shard_map/ppermute | solution.py:30
  88.7 5.3 %collective-permute-start.6 = (bf16[64,1024]{1,0:T(8,128)(2,1)S(1)}, bf16[64,1024]{1,0:T(8,128)(2,1)S(1)}, u32[]{:S(2)}, u32[]{:S(2)}) collective-permute-start(bf16[64,1024]{1,0:T(8,128)(2,1)S(1)} %collective-permute-done.5), channel_id=1, source_target_pairs={{4,0},{8,4},{12,8},{16,12},{20,16},{24,20},{28,24},{0,28},{5,1},{9... | collective-permute-start | bytes 393224 | tf_op jit(solution)/shard_map/ppermute | solution.py:30
  94.0 0.0 collective-permute-done.3
  94.1 2.4 %collective-permute-done.6 = bf16[64,1024]{1,0:T(8,128)(2,1)S(1)} collective-permute-done((bf16[64,1024]{1,0:T(8,128)(2,1)S(1)}, bf16[64,1024]{1,0:T(8,128)(2,1)S(1)}, u32[]{:S(2)}, u32[]{:S(2)}) %collective-permute-start.6) | collective-permute-done | bytes 131104 | tf_op jit(solution)/shard_map/ppermute | solution.py:30
  96.5 0.6 gather_fusion
  97.1 0.1 fusion.49
  97.2 0.2 copy.50
  97.4 0.2 copy.51
  97.6 0.9 fusion.1
  98.6 1.3 %fusion.2 = f32[4,8,64]{2,1,0:T(8,128)S(1)} fusion(f32[4,512,64,8]{1,2,3,0:T(8,128)S(1)} %get-tuple-element.46, f32[4,8,64]{2,1,0:T(8,128)S(1)} %get-tuple-element.31, pred[64,512]{1,0:T(8,128)(4,1)S(1)} %fusion.16), kind=kLoop, calls=%fused_computation.7 | loop fusion | flops 5240832 | bytes 4243456 | tf_op jit(solution)/shard_map/while/body/eval_jaxpr/reduce_sum | solution.py:167
  100.0 1.6 %fusion.19 = bf16[64,4,8,128]{3,0,2,1:T(8,128)(2,1)S(1)} fusion(bf16[512,4,128,1]{0,2,3,1:T(8,128)(2,1)S(1)} %bitcast.108, f32[4,512,64,8]{1,2,3,0:T(8,128)S(1)} %get-tuple-element.46, f32[4,8,64]{2,1,0:T(8,128)S(1)} %get-tuple-element.31, pred[64,512]{1,0:T(8,128)(4,1)S(1)} %fusion.16, f32[64,4,8]{0,2,1:T(8,128)S(1)} %bitcast_add_fusion, ...), kind=kOutput, calls=%fused_computation.29 | convolution fusion | flops 273416192 | bytes 5300224 | tf_op jit(solution)/shard_map/while/body/eval_jaxpr/hgqk,khd->hgqd/dot_general | solution.py:168
  101.6 0.3 copy.42
  101.9 0.2 reshape.373
  102.2 1.0 select_convert_fusion
  (30 shorter events, 0.4 us)
Async XLA Ops:
  7.2 22.2 %copy-start = (bf16[2048,128]{1,0:T(8,128)(2,1)S(1)}, bf16[2048,128]{1,0:T(8,128)(2,1)}, u32[]{:S(2)}) copy-start(bf16[2048,128]{1,0:T(8,128)(2,1)} %param.11) | copy-start | bytes 1572868
  7.2 8.4 %copy-start.3 = (s32[4,16]{1,0:T(4,128)S(1)}, s32[4,16]{1,0:T(4,128)}, u32[]{:S(2)}) copy-start(s32[4,16]{1,0:T(4,128)} %param.15) | copy-start | bytes 772
  10.7 18.7 %all-to-all-start = ((bf16[64,4,2048]{2,0,1:T(8,128)(2,1)}), bf16[64,4,2048]{2,0,1:T(8,128)(2,1)S(1)}, u32[]{:S(2)}, u32[]{:S(2)}) async-start(bf16[64,4,2048]{2,0,1:T(8,128)(2,1)} %copy.35), calls=%async_computation | async-start | bytes 2097152 | tf_op jit(solution)/shard_map/all_to_all | solution.py:100
  14.9 42.6 %reduce-scatter.2.cloned.1.call-start = ((), (), s32[]{:S(2)}) async-start(), calls=%async_computation.3 | async-start | bytes 737280 | tf_op jit(solution)/shard_map/reduce_scatter | solution.py:101
  29.8 4.5 %copy-start.4 = (s32[1,4,4]{2,1,0:T(4,128)S(1)}, s32[1,4,4]{2,1,0:T(4,128)}, u32[]{:S(2)}) copy-start(s32[1,4,4]{2,1,0:T(4,128)} %param.13) | copy-start | bytes 196
  29.8 28.6 %copy-start.2 = (bf16[2,64,512]{2,1,0:T(8,128)(2,1)S(1)}, bf16[2,64,512]{2,1,0:T(8,128)(2,1)}, u32[]{:S(2)}) copy-start(bf16[2,64,512]{2,1,0:T(8,128)(2,1)} %param.12) | copy-start | bytes 393220
  33.3 35.3 %copy-start.1 = (bf16[1,64,4096]{2,1,0:T(8,128)(2,1)S(1)}, bf16[1,64,4096]{2,1,0:T(8,128)(2,1)}, u32[]{:S(2)}) copy-start(bf16[1,64,4096]{2,1,0:T(8,128)(2,1)} %param.9) | copy-start | bytes 1572868
  60.6 8.0 %collective-permute-start = (bf16[64,1024]{1,0:T(8,128)(2,1)S(1)}, bf16[64,1024]{1,0:T(8,128)(2,1)S(1)}, u32[]{:S(2)}, u32[]{:S(2)}) collective-permute-start(bf16[64,1024]{1,0:T(8,128)(2,1)S(1)} %maximum_convert_fusion), channel_id=1, source_target_pairs={{0,4},{4,8},{8,12},{12,16},{16,20},{20,24},{24,28},{28,0},{1,5},{5... | collective-permute-start | bytes 393224 | tf_op jit(solution)/shard_map/ppermute | solution.py:28
  68.5 7.8 %collective-permute-start.1 = (bf16[64,1024]{1,0:T(8,128)(2,1)S(1)}, bf16[64,1024]{1,0:T(8,128)(2,1)S(1)}, u32[]{:S(2)}, u32[]{:S(2)}) collective-permute-start(bf16[64,1024]{1,0:T(8,128)(2,1)S(1)} %collective-permute-done), channel_id=1, source_target_pairs={{0,4},{4,8},{8,12},{12,16},{16,20},{20,24},{24,28},{28,0},{1,5},{5... | collective-permute-start | bytes 393224 | tf_op jit(solution)/shard_map/ppermute | solution.py:28
  69.1 11.4 %collective-permute-start.4 = (bf16[64,1024]{1,0:T(8,128)(2,1)S(1)}, bf16[64,1024]{1,0:T(8,128)(2,1)S(1)}, u32[]{:S(2)}, u32[]{:S(2)}) collective-permute-start(bf16[64,1024]{1,0:T(8,128)(2,1)S(1)} %maximum_convert_fusion), channel_id=1, source_target_pairs={{4,0},{8,4},{12,8},{16,12},{20,16},{24,20},{28,24},{0,28},{5,1},{9... | collective-permute-start | bytes 393224 | tf_op jit(solution)/shard_map/ppermute | solution.py:30
  76.3 9.0 %collective-permute-start.2 = (bf16[64,1024]{1,0:T(8,128)(2,1)S(1)}, bf16[64,1024]{1,0:T(8,128)(2,1)S(1)}, u32[]{:S(2)}, u32[]{:S(2)}) collective-permute-start(bf16[64,1024]{1,0:T(8,128)(2,1)S(1)} %collective-permute-done.1), channel_id=1, source_target_pairs={{0,4},{4,8},{8,12},{12,16},{16,20},{20,24},{24,28},{28,0},{1,5},{5... | collective-permute-start | bytes 393224 | tf_op jit(solution)/shard_map/ppermute | solution.py:28
  77.1 8.2 %all-to-all-start.1 = ((bf16[4,4,4096]{2,1,0:T(4,128)(2,1)}), bf16[4,4,4096]{2,1,0:T(4,128)(2,1)S(1)}, u32[]{:S(2)}, u32[]{:S(2)}) async-start(bf16[4,4,4096]{2,1,0:T(4,128)(2,1)} %convolution_convert_fusion), calls=%async_computation.2 | async-start | bytes 262144 | tf_op jit(solution)/shard_map/all_to_all | solution.py:67
  80.5 8.1 %collective-permute-start.5 = (bf16[64,1024]{1,0:T(8,128)(2,1)S(1)}, bf16[64,1024]{1,0:T(8,128)(2,1)S(1)}, u32[]{:S(2)}, u32[]{:S(2)}) collective-permute-start(bf16[64,1024]{1,0:T(8,128)(2,1)S(1)} %collective-permute-done.4), channel_id=1, source_target_pairs={{4,0},{8,4},{12,8},{16,12},{20,16},{24,20},{28,24},{0,28},{5,1},{9... | collective-permute-start | bytes 393224 | tf_op jit(solution)/shard_map/ppermute | solution.py:30
  85.3 8.7 %collective-permute-start.3 = (bf16[64,1024]{1,0:T(8,128)(2,1)S(1)}, bf16[64,1024]{1,0:T(8,128)(2,1)S(1)}, u32[]{:S(2)}, u32[]{:S(2)}) collective-permute-start(bf16[64,1024]{1,0:T(8,128)(2,1)S(1)} %collective-permute-done.2), channel_id=1, source_target_pairs={{0,4},{4,8},{8,12},{12,16},{16,20},{20,24},{24,28},{28,0},{1,5},{5... | collective-permute-start | bytes 393224 | tf_op jit(solution)/shard_map/ppermute | solution.py:28
  88.7 7.8 %collective-permute-start.6 = (bf16[64,1024]{1,0:T(8,128)(2,1)S(1)}, bf16[64,1024]{1,0:T(8,128)(2,1)S(1)}, u32[]{:S(2)}, u32[]{:S(2)}) collective-permute-start(bf16[64,1024]{1,0:T(8,128)(2,1)S(1)} %collective-permute-done.5), channel_id=1, source_target_pairs={{4,0},{8,4},{12,8},{16,12},{20,16},{24,20},{28,24},{0,28},{5,1},{9... | collective-permute-start | bytes 393224 | tf_op jit(solution)/shard_map/ppermute | solution.py:30
Sparse Core Ops, SparseCore 0:
  34.3 23.1 reduce-scatter.1
